TPU v7x, 128 devices: a whole 4x4x4 slice. The times are simulated.
128 devices in a mesh: gx: 4 (over x), gy: 4 (over z), gz: 8 (over y, core).
Axes of the slice: x: 4, y: 4, z: 4, core: 2. Of those that a mesh axis runs over, the one named last changes fastest.
Arguments:
- element_load: float32 [36, 36, 72, 128], P('gx', 'gy', 'gz'), may hold values from -90 to 90
- local_matrix: float32 [4, 4, 8, 729, 729], P('gx', 'gy', 'gz'), may hold values from -10 to 61, as said below
- dirichlet_inverse: float32 [4, 4, 8, 343, 343], P('gx', 'gy', 'gz'), as said below
- neumann_inverse: float32 [4, 4, 8, 729, 729], P('gx', 'gy', 'gz'), as said below
- coarse_basis: float32 [4, 4, 8, 20, 729], P('gx', 'gy', 'gz'), as said below
Outputs:
- solution: float32 [36, 36, 72, 128], P('gx', 'gy', 'gz')
- residual: float32 [36, 36, 72, 128], P('gx', 'gy', 'gz')
Inputs may be any that keep to these rules, and one draw needn't show every extreme that they name: `local_matrix`: block (a, b, c) is the symmetric positive definite stiffness matrix of subdomain (a, b, c) in the node order of the steps: cellwise conductivities on the couplings of neighbouring nodes plus a lumped reaction term. `dirichlet_inverse`: block (a, b, c) is the inverse, computed in float32, of local_matrix's block restricted to the inner nodes. `neumann_inverse`: block (a, b, c) is the node-by-node block of the inverse, computed in float32, of the saddle-point matrix [[A, Cm^T], [Cm, 0]], with A local_matrix's block and Cm the 20 x 729 primal constraints in the order of the coarse numbering: the value at each of the 8 corners, then the mean over the 7 inner nodes of each of the 12 edges. `coarse_basis`: block (a, b, c) is the constraint-by-node block of that same saddle-point inverse.
All inputs are finite; a program needn't handle non-finite values.
Results may differ from a plain program's by a relative error of at most 0.0014.
Values sent between devices are 32-bit elements; how exact they have to be, the bound alone decides.
A program may use at most 128 MiB of HBM per device.

v0:
```python
import functools

import jax
import jax.numpy as jnp
import numpy as np
from jax import lax
from jax.experimental import pallas as pl
from jax.experimental.pallas import tpu as pltpu
from jax.sharding import PartitionSpec as P

MESH = pl.DeviceIdType.MESH
F32, BF16 = jnp.float32, jnp.bfloat16
GX, GY, GZ = 4, 4, 8
M = 9
NODES, NB, NI, RHS = 729, 392, 343, 128
ORDER = (1, 3, 5, 7, 2, 6, 0, 4)
VM = pl.BlockSpec(memory_space=pltpu.VMEM)

_g = np.indices((M, M, M)).reshape(3, -1)
_rim = ((_g == 0) | (_g == M - 1)).sum(0)
B_IDS, I_IDS = np.where(_rim > 0)[0], np.where(_rim == 0)[0]
B_POS = {int(n): r for r, n in enumerate(B_IDS)}
I_POS = {int(n): r for r, n in enumerate(I_IDS)}


def one_hot(rows, cols, shape):
    out = np.zeros(shape, np.float32)
    out[rows, cols] = 1.0
    return out


B_COL = np.full((NB, 1), -1, np.int32)
B_COL[: len(B_IDS), 0] = B_IDS
I_COL = I_IDS.astype(np.int32)[:, None]
RUNS, _r = [], 0
while _r < len(B_IDS):
    _e = _r + 1
    while _e < len(B_IDS) and B_IDS[_e] == B_IDS[_e - 1] + 1:
        _e += 1
    RUNS.append((_r, int(B_IDS[_r]), _e - _r))
    _r = _e
WEIGHT = np.zeros((NB, 1), np.float32)
WEIGHT[: len(B_IDS), 0] = 1.0 / 2.0 ** _rim[B_IDS]
WEIGHT = np.broadcast_to(WEIGHT, (NB, RHS)).copy()

DIRS = sorted(
    ((x, y, z) for x in (-1, 0, 1) for y in (-1, 0, 1) for z in (-1, 0, 1) if (x, y, z) != (0, 0, 0)),
    key=lambda d: (sum(map(abs, d)), d),
)
SIZE = {1: 88, 2: 16, 3: 8}
OFFS, _at = {}, 0
for _d in DIRS:
    OFFS[_d] = (_at, SIZE[sum(map(abs, _d))])
    _at += OFFS[_d][1]
NS, NF = _at, 6 * SIZE[1]
K_COL = np.full((NS, 1), -1, np.int32)
for _d in DIRS:
    _sel = [[0] if v == -1 else [M - 1] if v == 1 else list(range(M)) for v in _d]
    for _r, (_i, _j, _k) in enumerate((i, j, k) for i in _sel[0] for j in _sel[1] for k in _sel[2]):
        K_COL[OFFS[_d][0] + _r, 0] = B_POS[(_i * M + _j) * M + _k]

CORNERS = [(x, y, z) for x in (0, 1) for y in (0, 1) for z in (0, 1)]
PRIM = [(0, o) for o in CORNERS]
PRIM += [(1, (0, y, z)) for y in (0, 1) for z in (0, 1)]
PRIM += [(2, (x, 0, z)) for x in (0, 1) for z in (0, 1)]
PRIM += [(3, (x, y, 0)) for x in (0, 1) for y in (0, 1)]
S64 = one_hot([CORNERS.index(o) * 8 + t for t, o in PRIM], np.arange(20), (64, 24))
TILE = np.tile(np.eye(24, dtype=np.float32), (1, 8))
TMASK = (np.arange(64)[:, None] // 8 == np.arange(192)[None, :] // 24).astype(np.float32)
SPREAD = np.zeros((192, 128), np.float32)
for _c, _o1 in enumerate(CORNERS):
    for _q, (_t, _o2) in enumerate(PRIM):
        _f = [b - a + 1 for a, b in zip(_o1, _o2)]
        SPREAD[_c * 24 + _q, _t * 27 + (_f[0] * 3 + _f[1]) * 3 + _f[2]] = 1.0


def dot(a, b, ca=1, cb=0):
    return lax.dot_general(
        a, b, (((ca,), (cb,)), ((), ())), precision=lax.Precision.HIGHEST, preferred_element_type=F32
    )


def pieces(x):
    h = x.astype(BF16)
    r = x - h.astype(F32)
    m = r.astype(BF16)
    return h, m, (r - m.astype(F32)).astype(BF16)


def mm(a, b, ca=1, cb=0):
    return lax.dot_general(a, b, (((ca,), (cb,)), ((), ())), preferred_element_type=F32)


def pick(sel, x):
    h, m, l = pieces(x)
    if x.shape[1] > 128:
        return mm(sel, h) + mm(sel, m) + mm(sel, l)
    n = x.shape[1]
    d = mm(sel, jnp.concatenate([h, m], axis=1))
    return d[:, :n] + d[:, n:] + mm(sel, l)


def pick_cols(x, sel):
    h, m, l = pieces(x)
    return mm(h, sel, 1, 1) + mm(m, sel, 1, 1) + mm(l, sel, 1, 1)


def dot6(a, b):
    b1, b2, b3 = pieces(b)
    n = b.shape[1]
    b12 = jnp.concatenate([b1, b2], axis=1)
    d = mm(a[1], b12) + mm(a[0], b12)
    return (mm(a[0], b3) + mm(a[2], b1)) + d[:, n:] + d[:, :n]


def here():
    return lax.axis_index("gx"), lax.axis_index("gy"), lax.axis_index("gz")


def at(d):
    x, y, z = here()
    return (lax.rem(x + d[0] + GX, GX), lax.rem(y + d[1] + GY, GY), lax.rem(z + d[2] + GZ, GZ))


PLANE = [(x, y, 0) for x in range(GX) for y in range(GY) if (x, y) != (0, 0)]
LINE = [(0, 0, z) for z in range(1, GZ)]
_norm = lambda d: (d[0] % GX, d[1] % GY, d[2] % GZ)
PARTNERS = sorted({_norm(d) for d in DIRS + PLANE + LINE})


def remote(src, dst, sems, k, d):
    return pltpu.make_async_remote_copy(
        src_ref=src, dst_ref=dst, send_sem=sems.at[2 * k], recv_sem=sems.at[2 * k + 1], device_id=at(d), device_id_type=MESH
    )


def exchange_start(send, recv, sems, k, faces):
    for d in DIRS:
        if (sum(map(abs, d)) == 1) == faces:
            o, n = OFFS[d]
            o2, _ = OFFS[tuple(-v for v in d)]
            remote(send.at[pl.ds(o, n)], recv.at[pl.ds(o2, n)], sems, k, d).start()


FACE_ROWS, REST_ROWS = pl.ds(0, NF), pl.ds(NF, NS - NF)


def swap_start(v, pk, send, recv, sems, k):
    send[REST_ROWS, :] = pick(pk[NF:], v)
    exchange_start(send, recv, sems, k + 1, False)
    send[FACE_ROWS, :] = pick(pk[:NF], v)
    exchange_start(send, recv, sems, k, True)


def swap_finish(v, pkt, send, recv, sems, k):
    bulk_wait(send.at[FACE_ROWS], recv.at[FACE_ROWS], sems, k)
    v = v + pick(pkt[:, :NF], recv[FACE_ROWS, :])
    bulk_wait(send.at[REST_ROWS], recv.at[REST_ROWS], sems, k + 1)
    return v + pick(pkt[:, NF:], recv[REST_ROWS, :])


def bulk_wait(send, recv, sems, k):
    c = remote(send, recv, sems, k, (1, 0, 0))
    c.wait_recv()
    c.wait_send()


def owner_start(send, recv, sems, k):
    for c, o in enumerate(CORNERS):
        if c:
            remote(send.at[pl.ds(8 * c, 8)], recv.at[pl.ds(8 * c, 8)], sems, k, o).start()


def owner_finish(send, recv, sems, k):
    bulk_wait(send.at[pl.ds(8, 56)], recv.at[pl.ds(8, 56)], sems, k)
    out = send[pl.ds(0, 8), :]
    for c in range(1, 8):
        out = out + recv[pl.ds(8 * c, 8), :]
    return out


def gather_start(val, plane, sems, k):
    x, y, _ = here()
    ab = x * GY + y
    odd = lax.rem(y, 2) == 1
    plane[ab] = jnp.where(jnp.full((8, 128), odd), pltpu.roll(val, 4, 0), val)
    for d in PLANE:
        remote(plane.at[ab], plane.at[ab], sems, k, d).start()


def gather_turn(plane, full, sems, k):
    bulk_wait(plane.at[pl.ds(0, 15)], plane.at[pl.ds(0, 15)], sems, k)
    _, _, z = here()
    pos = place(z)
    rows = [plane[2 * i] + plane[2 * i + 1] for i in range(8)]
    mine = pl.ds(pl.multiple_of(pos * 64, 64), 64)
    full[mine, :] = jnp.concatenate(rows, axis=0)
    for d in LINE:
        remote(full.at[mine], full.at[mine], sems, k + 1, d).start()


def gather_finish(full, sems, k):
    bulk_wait(full.at[pl.ds(0, 448)], full.at[pl.ds(0, 448)], sems, k + 1)


def reduce_start(val, plane, sems, k):
    x, y, _ = here()
    ab = x * GY + y
    plane[ab] = val
    for d in PLANE:
        remote(plane.at[ab], plane.at[ab], sems, k, d).start()


def reduce_turn(plane, line, sems, k):
    bulk_wait(plane.at[pl.ds(0, 15)], plane.at[pl.ds(0, 15)], sems, k)
    _, _, z = here()
    line[z] = jnp.sum(plane[...], axis=0)
    for d in LINE:
        remote(line.at[z], line.at[z], sems, k + 1, d).start()


def reduce_finish(line, sems, k):
    bulk_wait(line.at[pl.ds(0, 7)], line.at[pl.ds(0, 7)], sems, k + 1)
    return jnp.sum(line[...], axis=0)


SPLIT = []
for _i in range(M):
    for _j in range(M):
        _n = (_i * M + _j) * M
        if _i in (0, M - 1) or _j in (0, M - 1):
            SPLIT.append((_i, _j, [(False, 0, B_POS[_n], M)]))
        else:
            SPLIT.append((_i, _j, [(False, 0, B_POS[_n], 1), (True, 1, I_POS[_n + 1], M - 2), (False, M - 1, B_POS[_n + M - 1], 1)]))


def choose(ids_ref, n):
    ids = ids_ref[...]
    return (lax.broadcasted_iota(jnp.int32, (ids.shape[0], n), 1) == ids).astype(F32).astype(BF16)


def place(z):
    h = z // 2
    return lax.rem(z, 2) * h + (1 - lax.rem(z, 2)) * (6 - 2 * lax.rem(h, 2) + h // 2)


def coords(m):
    pos = m >> 6
    c = jnp.where(pos < 4, 2 * pos + 1, jnp.where(pos < 6, 4 * pos - 14, 4 * pos - 24))
    return (m >> 4) & 3, (m >> 2) & 3, c, m & 3


def build_coarse(kall_ref, kc):
    kall = kall_ref[...]
    ra, rb, rc, _ = coords(lax.broadcasted_iota(jnp.int32, (512, 128), 0))
    for j in range(4):
        ca, cb, cc, ct = coords(lax.broadcasted_iota(jnp.int32, (1, 128), 1) + 128 * j)
        da, db, dc = (ca + 1 - ra) & 3, (cb + 1 - rb) & 3, (cc + 1 - rc) & 7
        hit = (da < 3) & (db < 3) & (dc < 3)
        slot = jnp.where(hit, ct * 27 + da * 9 + db * 3 + dc, 0)
        v = jnp.take_along_axis(kall, slot, axis=1, mode="promise_in_bounds")
        kc[:, pl.ds(128 * j, 128)] = jnp.where(hit, v, 0.0)


def sweep(ref, n):
    lane = lax.broadcasted_iota(jnp.int32, (n, 128), 1)
    base = lane // n * n
    take = lambda v, idx: jnp.take_along_axis(v, idx, axis=1, mode="promise_in_bounds")

    def body(i, carry):
        k = 2 * i
        i0, i1 = base + k, base + k + 1
        s0, s1 = i0[0:8], i1[0:8]
        for j in range(ref.shape[0]):
            x = ref[j]
            r0 = jnp.broadcast_to(ref[j, pl.ds(k, 1), :], (8, 128))
            r1 = jnp.broadcast_to(ref[j, pl.ds(k + 1, 1), :], (8, 128))
            c0, c1 = take(x, i0), take(x, i1)
            p, q, r = take(r0, s0), take(r0, s1), take(r1, s1)
            d = 1.0 / (p * r - q * q)
            b00, b01, b11 = r * d, -q * d, p * d
            on0, on1 = lane[0:8] == s0, lane[0:8] == s1
            n0 = jnp.where(on0, b00, jnp.where(on1, b01, b00 * r0 + b01 * r1))
            n1 = jnp.where(on0, b01, jnp.where(on1, b11, b01 * r0 + b11 * r1))
            left = jnp.where((lane == i0) | (lane == i1), 0.0, x)
            ref[j] = left - c0 * n0[0:1] - c1 * n1[0:1]
            ref[j, pl.ds(k, 1), :] = n0[0:1]
            ref[j, pl.ds(k + 1, 1), :] = n1[0:1]
        return carry

    lax.fori_loop(0, n // 2, body, 0)


def program(load_h, a_h, di_h, n_h, phi_h, bcol, icol, kcol, krow, wt_ref, s64_ref, tile_ref, tmask_ref, spread_ref,
            xb_ref, xi_ref, rb_ref, ri_ref,
            load_v, a_v, n_v, arows, nrows, di_v, phi_v, lb_v, li_v, send, recv, ssend, srecv,
            ksend, krecv, hsend, hrecv, kplane, gplane, kfull, gfull, rplane, rline, kc, xo, x2, xf, sems, dsems):
    sem = pltpu.get_barrier_semaphore()
    for d in PARTNERS:
        pl.semaphore_signal(sem, inc=1, device_id=at(d), device_id_type=MESH)

    get_phi = pltpu.make_async_copy(phi_h.at[:, 0, :], phi_v, dsems.at[0])
    get_load = pltpu.make_async_copy(load_h, load_v, dsems.at[1])
    get_di = pltpu.make_async_copy(di_h.at[:, 0, :], di_v, dsems.at[2])
    get_phi.start()
    get_a = pltpu.make_async_copy(a_h.at[:, 0, :], a_v, dsems.at[3])
    get_n = pltpu.make_async_copy(n_h.at[:, 0, :], n_v, dsems.at[4])
    get_a.start()
    get_load.start()
    get_di.start()
    get_n.start()

    def border_rows(src, dst):
        dst[pl.ds(NB - 8, 8), :] = jnp.zeros((8, NODES), F32)
        for r, n, c in RUNS:
            dst[pl.ds(r, c), :] = src[pl.ds(n, c), :]

    pb, pi, pk = choose(bcol, NODES), choose(icol, NODES), choose(kcol, NB)
    pkt = (lax.broadcasted_iota(jnp.int32, (NB, NS), 0) == krow[...]).astype(F32).astype(BF16)
    wt = wt_ref[...]

    get_phi.wait()
    phi = jnp.concatenate([phi_v[...], jnp.zeros((4, NODES), F32)], axis=0)
    p24 = pick_cols(phi, pb)
    get_a.wait()
    border_rows(a_v, arows)
    ab = arows[...]
    k24 = dot(p24, dot(ab, phi, 1, 1))
    k64 = dot(dot(s64_ref[...], k24), tile_ref[...]) * tmask_ref[...]
    ksend[...] = dot(k64, spread_ref[...])
    pl.semaphore_wait(sem, len(PARTNERS))
    owner_start(ksend, krecv, sems, 0)

    get_load.wait()
    lb_v[pl.ds(NB - 8, 8), :] = jnp.zeros((8, RHS), F32)
    for i, j, parts in SPLIT:
        for inner, k, r, c in parts:
            (li_v if inner else lb_v)[pl.ds(r, c), :] = load_v[i, j, pl.ds(k, c), :]
    lb, li = lb_v[...], li_v[...]
    get_di.wait()
    di = di_v[...]
    start = dot(di, li)
    abi = pick_cols(ab, pi)
    c = lb - dot(abi, start)
    cl = jnp.concatenate([c, lb], axis=1)
    swap_start(cl, pk, send, recv, sems, 18)
    gather_start(owner_finish(ksend, krecv, sems, 0), kplane, sems, 2)
    k0 = jnp.sum(li * start, axis=0, keepdims=True)
    x = dot(di, abi, 1, 1)
    asm = swap_finish(cl, pkt, send, recv, sems, 18)
    f = wt * asm[:, 0:RHS]
    hsend[0] = dot(s64_ref[...], dot(p24, f))
    owner_start(hsend.at[0], hrecv.at[0], sems, 4)
    gather_turn(kplane, kfull, sems, 2)
    s = pieces(pick_cols(ab, pb) - dot(abi, x))
    get_n.wait()
    border_rows(n_v, nrows)
    nbb = pieces(pick_cols(nrows[...], pb))
    w = dot6(nbb, f)
    gather_start(owner_finish(hsend.at[0], hrecv.at[0], sems, 4), gplane.at[0], sems, 5)
    gather_finish(kfull, sems, 2)

    build_coarse(kfull, kc)
    low = lax.broadcasted_iota(jnp.int32, (64, 128), 1) < 64
    for j in range(2):
        cut = pl.ds(128 * j, 128)
        xo[j] = jnp.where(low, kc[pl.ds(128 * j, 64), cut], kc[pl.ds(128 * j + 64, 64), cut])
    sweep(xo, 64)
    gather_turn(gplane.at[0], gfull.at[0], sems, 5)
    group = lax.broadcasted_iota(jnp.int32, (64, 256), 1) // 64
    both = jnp.concatenate([xo[0], xo[1]], axis=1)
    inv_o = jnp.concatenate([jnp.where(group == g, both, 0.0) for g in range(4)], axis=0)
    koe = kc[pl.ds(0, 256), pl.ds(256, 256)]
    m = dot(inv_o, koe)
    se = kc[pl.ds(256, 256), pl.ds(256, 256)] - dot(koe, m, 0, 0)
    x2[0] = jnp.where(low, se[0:64, 0:128], se[64:128, 0:128])
    sweep(x2, 64)
    inv_2 = jnp.concatenate([jnp.where(low, x2[0], 0.0), jnp.where(low, 0.0, x2[0])], axis=0)
    k2f = se[0:128, 128:256]
    m2 = dot(inv_2, k2f)
    xf[0] = se[128:256, 128:256] - dot(k2f, m2, 0, 0)
    sweep(xf, 128)
    prim = lax.broadcasted_iota(jnp.int32, (24, 512), 0)
    want = jnp.full((24, 512), -1, jnp.int32)
    for q, (t, o) in enumerate(PRIM):
        cx, cy, cz = at(o)
        want = jnp.where(prim == q, place(cz) * 64 + (cx * GY + cy) * 4 + t, want)
    sel = (want == lax.broadcasted_iota(jnp.int32, (24, 512), 1)).astype(F32)
    so = sel[:, 0:256]
    s_e = sel[:, 256:512] - dot(so, m)
    s_2 = s_e[:, 0:128]
    wf = dot(s_e[:, 128:256] - dot(s_2, m2), xf[0])
    w2 = dot(s_2, inv_2) - dot(wf, m2, 1, 1)
    we = jnp.concatenate([w2, wf], axis=1)
    w24 = jnp.concatenate([dot(so, inv_o) - dot(we, m, 1, 1), we], axis=1)

    def apply_coarse(w, g):
        return wt * (w + dot(p24, dot(w24, g), 0, 0))

    part = lambda a, b: jnp.sum(a * b, axis=0, keepdims=True)
    gather_finish(gfull.at[0], sems, 5)
    u = apply_coarse(w, gfull[0])
    swap_start(u, pk, ssend.at[0], srecv.at[0], sems, 20)
    z1 = swap_finish(u, pkt, ssend.at[0], srecv.at[0], sems, 20)
    t1 = dot6(s, z1)
    swap_start(t1, pk, ssend.at[1], srecv.at[1], sems, 22)
    reduce_start(jnp.concatenate([k0, part(c, z1), part(z1, t1), jnp.zeros((5, RHS), F32)], axis=0), rplane.at[0], sems, 11)
    at1 = swap_finish(t1, pkt, ssend.at[1], srecv.at[1], sems, 22)
    f = wt * at1
    hsend[1] = dot(s64_ref[...], dot(p24, f))
    owner_start(hsend.at[1], hrecv.at[1], sems, 13)
    w = dot6(nbb, f)
    reduce_turn(rplane.at[0], rline.at[0], sems, 11)
    gather_start(owner_finish(hsend.at[1], hrecv.at[1], sems, 13), gplane.at[1], sems, 14)
    gather_turn(gplane.at[1], gfull.at[1], sems, 14)
    sums = reduce_finish(rline.at[0], sems, 11)
    k0s = sums[0:1]
    g0 = k0s + sums[1:2]
    s1 = g0 / (k0s + sums[2:3])
    gather_finish(gfull.at[1], sems, 14)
    u = apply_coarse(w, gfull[1])
    swap_start(u, pk, ssend.at[2], srecv.at[2], sems, 24)
    z2 = swap_finish(u, pkt, ssend.at[2], srecv.at[2], sems, 24)
    t2 = dot6(s, z2)
    swap_start(t2, pk, ssend.at[3], srecv.at[3], sems, 26)
    zp, tp, cp = z1 - s1 * z2, t1 - s1 * t2, c - s1 * t1
    reduce_start(jnp.concatenate([part(cp, zp), part(zp, tp), jnp.zeros((6, RHS), F32)], axis=0), rplane.at[1], sems, 16)
    at2 = swap_finish(t2, pkt, ssend.at[3], srecv.at[3], sems, 26)
    reduce_turn(rplane.at[1], rline.at[1], sems, 16)
    last = reduce_finish(rline.at[1], sems, 16)
    rest = 1.0 - s1
    g1 = rest * rest * k0s + last[0:1]
    beta = g1 / g0
    s2 = g1 / (rest * rest * k0s + last[1:2] - beta * g1 / s1)

    xb = s1 * z1 + s2 * (zp + beta * z1)
    xi = (s1 + s2 * (rest + beta)) * start - dot(x, xb)
    kappa = rest * (1.0 - s2) - s2 * beta
    ac = asm[:, 0:RHS]
    ae = asm[:, RHS : 2 * RHS] - ac
    rb = kappa * ae + (ac - s1 * at1) - s2 * ((at1 - s1 * at2) + beta * at1)
    xb_ref[...], xi_ref[...] = xb, xi
    rb_ref[...], ri_ref[...] = rb, kappa * li


def spread(xb_ref, xi_ref, rb_ref, ri_ref, sol_ref, res_ref):
    for i, j, parts in SPLIT:
        for inner, k, r, c in parts:
            rows, there = pl.ds(r, c), pl.ds(k, c)
            sol_ref[i, j, there, :] = (xi_ref if inner else xb_ref)[rows, :]
            res_ref[i, j, there, :] = (ri_ref if inner else rb_ref)[rows, :]


def local(load, a, di, n, phi):
    tables = [jnp.asarray(v) for v in (B_COL, I_COL, K_COL, K_COL.T, WEIGHT, S64, TILE, TMASK, SPREAD)]
    V = lambda *s: pltpu.VMEM(s, F32)
    shape = jax.ShapeDtypeStruct((M, M, M, RHS), F32)
    half = [jax.ShapeDtypeStruct((NB, RHS), F32), jax.ShapeDtypeStruct((NI, RHS), F32)] * 2
    parts = pl.pallas_call(
        program,
        out_shape=half,
        in_specs=[pl.BlockSpec(memory_space=pl.ANY)] * 5 + [VM] * len(tables),
        out_specs=[VM] * 4,
        scratch_shapes=[
            V(M, M, M, RHS), V(NODES, NODES), V(NODES, NODES), V(NB, NODES), V(NB, NODES), V(NI, NI), V(20, NODES), V(NB, RHS), V(NI, RHS),
            V(NS, 2 * RHS), V(NS, 2 * RHS), V(4, NS, RHS), V(4, NS, RHS),
            V(64, 128), V(64, 128), V(2, 64, 128), V(2, 64, 128), V(16, 8, 128), V(2, 16, 8, 128), V(512, 128), V(2, 512, 128),
            V(2, 16, 8, 128), V(2, 8, 8, 128), V(512, 512), V(2, 64, 128), V(1, 64, 128), V(1, 128, 128),
            pltpu.SemaphoreType.DMA((56,)), pltpu.SemaphoreType.DMA((5,)),
        ],
        compiler_params=pltpu.CompilerParams(vmem_limit_bytes=60 * 2**20, collective_id=0, has_side_effects=True),
        name="program",
    )(load, a.reshape(NODES, 1, NODES), di.reshape(NI, 1, NI), n.reshape(NODES, 1, NODES), phi.reshape(20, 1, NODES), *tables)
    return tuple(pl.pallas_call(
        spread, out_shape=[shape, shape], in_specs=[VM] * 4, out_specs=[VM] * 2,
        compiler_params=pltpu.CompilerParams(vmem_limit_bytes=16 * 2**20), name="spread",
    )(*parts))


def solution(mesh):
    spec4, spec5 = P("gx", "gy", "gz", None), P("gx", "gy", "gz", None, None)
    return jax.shard_map(
        local, mesh=mesh, in_specs=(spec4, spec5, spec5, spec5, spec5), out_specs=(spec4, spec4), check_vma=False
    )
```

profile of v0, /device:TPU:1, one launch (start us, length us, event | category | flops | bytes accessed | tf_op | source)
XLA Modules:
  0.0 109.1 jit_solution(6441279019377018574)
XLA Ops:
  0.6 103.5 %program.1 = (f32[392,128]{1,0:T(8,128)}, f32[343,128]{1,0:T(8,128)}, f32[392,128]{1,0:T(8,128)}, f32[343,128]{1,0:T(8,128)}) custom-call(f32[9,9,9,128]{3,2,1,0:T(8,128)} %load_h.1, f32[729,1,729]{2,1,0:T(1,128)} %bitcast.4, f32[343,1,343]{2,1,0:T(1,128)} %bitcast.6, f32[729,1,729]{2,1,0:T(1,128)} %bitcast.5, f32[20,1,729]{2,1,0:T(1,128)} %bitcast.7, ...), custom_call_target="tpu_custom_call" | custom-call | tf_op jit(solution)/shard_map/program/pallas_call | solution.py:459
  104.2 0.0 copy-start
  104.2 0.9 copy-done
  105.1 0.0 copy-start.1
  105.1 0.9 copy-done.1
  106.0 0.0 copy-start.2
  106.0 0.9 copy-done.2
  106.9 0.0 copy-start.3
  106.9 0.9 copy-done.3
  107.9 1.2 %spread.1 = (f32[9,9,9,128]{3,2,1,0:T(8,128)}, f32[9,9,9,128]{3,2,1,0:T(8,128)}) custom-call(f32[392,128]{1,0:T(8,128)S(1)} %copy-done, f32[343,128]{1,0:T(8,128)S(1)} %copy-done.2, f32[392,128]{1,0:T(8,128)S(1)} %copy-done.1, f32[343,128]{1,0:T(8,128)S(1)} %copy-done.3), custom_call_target="tpu_custom_call" | custom-call | tf_op jit(solution)/shard_map/spread/pallas_call | solution.py:474
Async XLA Ops:
  104.2 0.9 copy-start
  105.1 0.9 copy-start.1
  106.0 0.9 copy-start.2
  106.9 0.9 copy-start.3
where the time goes:
time: 109 us
  Pallas kernels  105 us (96%)
  local copies, waits for them, and re-layouts  3.69 us (3%)
    pallas_call x1, Pallas kernels, local(): pl.pallas_call(program, out_shape=half, in_specs=[pl.BlockSpec(memory_spa...  104 us
    unnamed x8, local copies, waits for them, and re-layouts  3.69 us

commit v1 on v0

--- a/solution.py
+++ b/solution.py
@@ -65,7 +65,6 @@
 PRIM += [(2, (x, 0, z)) for x in (0, 1) for z in (0, 1)]
 PRIM += [(3, (x, y, 0)) for x in (0, 1) for y in (0, 1)]
 S64 = one_hot([CORNERS.index(o) * 8 + t for t, o in PRIM], np.arange(20), (64, 24))
-TILE = np.tile(np.eye(24, dtype=np.float32), (1, 8))
 TMASK = (np.arange(64)[:, None] // 8 == np.arange(192)[None, :] // 24).astype(np.float32)
 SPREAD = np.zeros((192, 128), np.float32)
 for _c, _o1 in enumerate(CORNERS):
@@ -111,6 +110,11 @@
     b12 = jnp.concatenate([b1, b2], axis=1)
     d = mm(a[1], b12) + mm(a[0], b12)
     return (mm(a[0], b3) + mm(a[2], b1)) + d[:, n:] + d[:, :n]
+
+
+def pick_right(x, sel):
+    h, m, l = pieces(x)
+    return mm(h, sel) + mm(m, sel) + mm(l, sel)
 
 
 def here():
@@ -268,31 +272,46 @@
     take = lambda v, idx: jnp.take_along_axis(v, idx, axis=1, mode="promise_in_bounds")
 
     def body(i, carry):
-        k = 2 * i
-        i0, i1 = base + k, base + k + 1
-        s0, s1 = i0[0:8], i1[0:8]
+        k = 4 * i
+        idx = [base + (k + q) for q in range(4)]
+        top = [v[0:8] for v in idx]
+        stored = []
         for j in range(ref.shape[0]):
             x = ref[j]
-            r0 = jnp.broadcast_to(ref[j, pl.ds(k, 1), :], (8, 128))
-            r1 = jnp.broadcast_to(ref[j, pl.ds(k + 1, 1), :], (8, 128))
-            c0, c1 = take(x, i0), take(x, i1)
-            p, q, r = take(r0, s0), take(r0, s1), take(r1, s1)
+            rows = [jnp.broadcast_to(ref[j, pl.ds(k + q, 1), :], (8, 128)) for q in range(4)]
+            a, b, c = take(rows[0], top[0]), take(rows[0], top[1]), take(rows[1], top[1])
+            e, f, g, h = take(rows[0], top[2]), take(rows[0], top[3]), take(rows[1], top[2]), take(rows[1], top[3])
+            p, q, r = take(rows[2], top[2]), take(rows[2], top[3]), take(rows[3], top[3])
+            cols = [take(x, v) for v in idx]
+            d = 1.0 / (a * c - b * b)
+            a, b, c = c * d, -b * d, a * d
+            we, wf, wg, wh = a * e + b * g, a * f + b * h, b * e + c * g, b * f + c * h
+            p, q, r = p - (e * we + g * wg), q - (e * wf + g * wh), r - (f * wf + h * wh)
             d = 1.0 / (p * r - q * q)
-            b00, b01, b11 = r * d, -q * d, p * d
-            on0, on1 = lane[0:8] == s0, lane[0:8] == s1
-            n0 = jnp.where(on0, b00, jnp.where(on1, b01, b00 * r0 + b01 * r1))
-            n1 = jnp.where(on0, b01, jnp.where(on1, b11, b01 * r0 + b11 * r1))
-            left = jnp.where((lane == i0) | (lane == i1), 0.0, x)
-            ref[j] = left - c0 * n0[0:1] - c1 * n1[0:1]
-            ref[j, pl.ds(k, 1), :] = n0[0:1]
-            ref[j, pl.ds(k + 1, 1), :] = n1[0:1]
+            p, q, r = r * d, -q * d, p * d
+            ue, uf, ug, uh = we * p + wf * q, we * q + wf * r, wg * p + wh * q, wg * q + wh * r
+            a, b, c = a + (ue * we + uf * wf), b + (ue * wg + uf * wh), c + (ug * wg + uh * wh)
+            inv = [[a, b, -ue, -uf], [b, c, -ug, -uh], [-ue, -ug, p, q], [-uf, -uh, q, r]]
+            on = [lane[0:8] == v for v in top]
+            new = []
+            for m in inv:
+                v = (m[0] * rows[0] + m[1] * rows[1]) + (m[2] * rows[2] + m[3] * rows[3])
+                for q in range(4):
+                    v = jnp.where(on[q], m[q], v)
+                new.append(v[0:1])
+            left = jnp.where((lane >= idx[0]) & (lane <= idx[3]), 0.0, x)
+            stored.append((left - (cols[0] * new[0] + cols[1] * new[1]) - (cols[2] * new[2] + cols[3] * new[3]), new))
+        for j, (v, new) in enumerate(stored):
+            ref[j] = v
+            for q in range(4):
+                ref[j, pl.ds(k + q, 1), :] = new[q]
         return carry
 
-    lax.fori_loop(0, n // 2, body, 0)
-
-
-def program(load_h, a_h, di_h, n_h, phi_h, bcol, icol, kcol, krow, wt_ref, s64_ref, tile_ref, tmask_ref, spread_ref,
-            xb_ref, xi_ref, rb_ref, ri_ref,
+    lax.fori_loop(0, n // 4, body, 0)
+
+
+def program(load_h, a_h, di_h, n_h, phi_h, bcol, icol, kcol, krow, wt_ref, s64_ref, tmask_ref, spread_ref,
+            parts_ref,
             load_v, a_v, n_v, arows, nrows, di_v, phi_v, lb_v, li_v, send, recv, ssend, srecv,
             ksend, krecv, hsend, hrecv, kplane, gplane, kfull, gfull, rplane, rline, kc, xo, x2, xf, sems, dsems):
     sem = pltpu.get_barrier_semaphore()
@@ -321,13 +340,14 @@
 
     get_phi.wait()
     phi = jnp.concatenate([phi_v[...], jnp.zeros((4, NODES), F32)], axis=0)
+    phi8 = jnp.concatenate([phi] * 8, axis=0)
     p24 = pick_cols(phi, pb)
+    p64 = pick(s64_ref[...].astype(BF16), p24)
     get_a.wait()
     border_rows(a_v, arows)
     ab = arows[...]
-    k24 = dot(p24, dot(ab, phi, 1, 1))
-    k64 = dot(dot(s64_ref[...], k24), tile_ref[...]) * tmask_ref[...]
-    ksend[...] = dot(k64, spread_ref[...])
+    k64 = dot(p64, dot(ab, phi8, 1, 1)) * tmask_ref[...]
+    ksend[...] = pick_right(k64, spread_ref[...].astype(BF16))
     pl.semaphore_wait(sem, len(PARTNERS))
     owner_start(ksend, krecv, sems, 0)
 
@@ -338,24 +358,22 @@
             (li_v if inner else lb_v)[pl.ds(r, c), :] = load_v[i, j, pl.ds(k, c), :]
     lb, li = lb_v[...], li_v[...]
     get_di.wait()
-    di = di_v[...]
-    start = dot(di, li)
+    start = dot6(pieces(di_v[...]), li)
     abi = pick_cols(ab, pi)
-    c = lb - dot(abi, start)
+    c = lb - dot6(pieces(abi), start)
     cl = jnp.concatenate([c, lb], axis=1)
     swap_start(cl, pk, send, recv, sems, 18)
     gather_start(owner_finish(ksend, krecv, sems, 0), kplane, sems, 2)
     k0 = jnp.sum(li * start, axis=0, keepdims=True)
-    x = dot(di, abi, 1, 1)
-    asm = swap_finish(cl, pkt, send, recv, sems, 18)
-    f = wt * asm[:, 0:RHS]
-    hsend[0] = dot(s64_ref[...], dot(p24, f))
-    owner_start(hsend.at[0], hrecv.at[0], sems, 4)
-    gather_turn(kplane, kfull, sems, 2)
-    s = pieces(pick_cols(ab, pb) - dot(abi, x))
+    p64 = pieces(p64)
     get_n.wait()
     border_rows(n_v, nrows)
     nbb = pieces(pick_cols(nrows[...], pb))
+    asm = swap_finish(cl, pkt, send, recv, sems, 18)
+    f = wt * asm[:, 0:RHS]
+    hsend[0] = dot6(p64, f)
+    owner_start(hsend.at[0], hrecv.at[0], sems, 4)
+    gather_turn(kplane, kfull, sems, 2)
     w = dot6(nbb, f)
     gather_start(owner_finish(hsend.at[0], hrecv.at[0], sems, 4), gplane.at[0], sems, 5)
     gather_finish(kfull, sems, 2)
@@ -401,13 +419,15 @@
     gather_finish(gfull.at[0], sems, 5)
     u = apply_coarse(w, gfull[0])
     swap_start(u, pk, ssend.at[0], srecv.at[0], sems, 20)
+    x = dot(di_v[...], abi, 1, 1)
+    s = pieces(pick_cols(ab, pb) - dot(abi, x))
     z1 = swap_finish(u, pkt, ssend.at[0], srecv.at[0], sems, 20)
     t1 = dot6(s, z1)
     swap_start(t1, pk, ssend.at[1], srecv.at[1], sems, 22)
     reduce_start(jnp.concatenate([k0, part(c, z1), part(z1, t1), jnp.zeros((5, RHS), F32)], axis=0), rplane.at[0], sems, 11)
     at1 = swap_finish(t1, pkt, ssend.at[1], srecv.at[1], sems, 22)
     f = wt * at1
-    hsend[1] = dot(s64_ref[...], dot(p24, f))
+    hsend[1] = dot6(p64, f)
     owner_start(hsend.at[1], hrecv.at[1], sems, 13)
     w = dot6(nbb, f)
     reduce_turn(rplane.at[0], rline.at[0], sems, 11)
@@ -425,6 +445,7 @@
     swap_start(t2, pk, ssend.at[3], srecv.at[3], sems, 26)
     zp, tp, cp = z1 - s1 * z2, t1 - s1 * t2, c - s1 * t1
     reduce_start(jnp.concatenate([part(cp, zp), part(zp, tp), jnp.zeros((6, RHS), F32)], axis=0), rplane.at[1], sems, 16)
+    xz = dot(x, jnp.concatenate([z1, zp], axis=1))
     at2 = swap_finish(t2, pkt, ssend.at[3], srecv.at[3], sems, 26)
     reduce_turn(rplane.at[1], rline.at[1], sems, 16)
     last = reduce_finish(rline.at[1], sems, 16)
@@ -434,33 +455,35 @@
     s2 = g1 / (rest * rest * k0s + last[1:2] - beta * g1 / s1)
 
     xb = s1 * z1 + s2 * (zp + beta * z1)
-    xi = (s1 + s2 * (rest + beta)) * start - dot(x, xb)
+    xi = (s1 + s2 * (rest + beta)) * start - (s1 + s2 * beta) * xz[:, :RHS] - s2 * xz[:, RHS:]
     kappa = rest * (1.0 - s2) - s2 * beta
     ac = asm[:, 0:RHS]
     ae = asm[:, RHS : 2 * RHS] - ac
     rb = kappa * ae + (ac - s1 * at1) - s2 * ((at1 - s1 * at2) + beta * at1)
-    xb_ref[...], xi_ref[...] = xb, xi
-    rb_ref[...], ri_ref[...] = rb, kappa * li
-
-
-def spread(xb_ref, xi_ref, rb_ref, ri_ref, sol_ref, res_ref):
+    parts_ref[pl.ds(AT[0], NB), :], parts_ref[pl.ds(AT[1], NI), :] = xb, xi
+    parts_ref[pl.ds(AT[2], NB), :], parts_ref[pl.ds(AT[3], NI), :] = rb, kappa * li
+
+
+AT = (0, NB, NB + 344, 2 * NB + 344)
+
+
+def spread(parts_ref, sol_ref, res_ref):
     for i, j, parts in SPLIT:
         for inner, k, r, c in parts:
-            rows, there = pl.ds(r, c), pl.ds(k, c)
-            sol_ref[i, j, there, :] = (xi_ref if inner else xb_ref)[rows, :]
-            res_ref[i, j, there, :] = (ri_ref if inner else rb_ref)[rows, :]
+            there = pl.ds(k, c)
+            sol_ref[i, j, there, :] = parts_ref[pl.ds(AT[inner] + r, c), :]
+            res_ref[i, j, there, :] = parts_ref[pl.ds(AT[2 + inner] + r, c), :]
 
 
 def local(load, a, di, n, phi):
-    tables = [jnp.asarray(v) for v in (B_COL, I_COL, K_COL, K_COL.T, WEIGHT, S64, TILE, TMASK, SPREAD)]
+    tables = [jnp.asarray(v) for v in (B_COL, I_COL, K_COL, K_COL.T, WEIGHT, S64, TMASK, SPREAD)]
     V = lambda *s: pltpu.VMEM(s, F32)
     shape = jax.ShapeDtypeStruct((M, M, M, RHS), F32)
-    half = [jax.ShapeDtypeStruct((NB, RHS), F32), jax.ShapeDtypeStruct((NI, RHS), F32)] * 2
     parts = pl.pallas_call(
         program,
-        out_shape=half,
+        out_shape=jax.ShapeDtypeStruct((2 * NB + 688, RHS), F32),
         in_specs=[pl.BlockSpec(memory_space=pl.ANY)] * 5 + [VM] * len(tables),
-        out_specs=[VM] * 4,
+        out_specs=VM,
         scratch_shapes=[
             V(M, M, M, RHS), V(NODES, NODES), V(NODES, NODES), V(NB, NODES), V(NB, NODES), V(NI, NI), V(20, NODES), V(NB, RHS), V(NI, RHS),
             V(NS, 2 * RHS), V(NS, 2 * RHS), V(4, NS, RHS), V(4, NS, RHS),
@@ -472,9 +495,9 @@
         name="program",
     )(load, a.reshape(NODES, 1, NODES), di.reshape(NI, 1, NI), n.reshape(NODES, 1, NODES), phi.reshape(20, 1, NODES), *tables)
     return tuple(pl.pallas_call(
-        spread, out_shape=[shape, shape], in_specs=[VM] * 4, out_specs=[VM] * 2,
+        spread, out_shape=[shape, shape], in_specs=[VM], out_specs=[VM] * 2,
         compiler_params=pltpu.CompilerParams(vmem_limit_bytes=16 * 2**20), name="spread",
-    )(*parts))
+    )(parts))
 
 
 def solution(mesh):

time: 109 us -> 96.6 us (0.89)
  Pallas kernels: 105 us -> 94.7 us
  local copies, waits for them, and re-layouts: 3.69 us -> 1.11 us
    pallas_call x2, Pallas kernels: 105 us -> 94.7 us  [the longest x1 93.5 us: local(): pl.pallas_call(program, out_shape=jax.ShapeDtypeStruct((2 * NB + 688, RHS...]
    unnamed x8 -> x2, local copies, waits for them, and re-layouts: 3.69 us -> 1.11 us
where the time goes in v1:
time: 96.6 us; the launch traced here: 96.5 us
  Pallas kernels  94.7 us (98%)
  local copies, waits for them, and re-layouts  1.11 us (1%)
    pallas_call x1, Pallas kernels, local(): pl.pallas_call(program, out_shape=jax.ShapeDtypeStruct((2 * NB + 688, RHS...  93.5 us

profile of v1, /device:TPU:1, one launch (start us, length us, event | category | flops | bytes accessed | tf_op | source)
XLA Modules:
  0.0 96.5 jit_solution(5019863272408742551)
XLA Ops:
  0.6 93.5 %program.1.parts_ref = f32[1472,128]{1,0:T(8,128)} custom-call(f32[9,9,9,128]{3,2,1,0:T(8,128)} %load_h.1, f32[729,1,729]{2,1,0:T(1,128)} %bitcast.4, f32[343,1,343]{2,1,0:T(1,128)} %bitcast.6, f32[729,1,729]{2,1,0:T(1,128)} %bitcast.5, f32[20,1,729]{2,1,0:T(1,128)} %bitcast.7, s32[392,1]{1,0:T(8,128)} %constant.16.clone.bcol, ...), custom_call_target="tpu_custom_call" | custom-call | tf_op jit(solution)/shard_map/program/pallas_call | solution.py:482
  94.2 0.0 copy-start
  94.2 1.1 %copy-done = f32[1472,128]{1,0:T(8,128)S(1)} copy-done((f32[1472,128]{1,0:T(8,128)S(1)}, f32[1472,128]{1,0:T(8,128)}, u32[]{:S(2)}) %copy-start) | copy-done | bytes 753688
  95.3 1.2 %spread.1 = (f32[9,9,9,128]{3,2,1,0:T(8,128)}, f32[9,9,9,128]{3,2,1,0:T(8,128)}) custom-call(f32[1472,128]{1,0:T(8,128)S(1)} %copy-done), custom_call_target="tpu_custom_call" | custom-call | tf_op jit(solution)/shard_map/spread/pallas_call | solution.py:497
Async XLA Ops:
  94.2 1.1 %copy-start = (f32[1472,128]{1,0:T(8,128)S(1)}, f32[1472,128]{1,0:T(8,128)}, u32[]{:S(2)}) copy-start(f32[1472,128]{1,0:T(8,128)} %program.1.parts_ref) | copy-start | bytes 2260996

commit v2 on v1

--- a/solution.py
+++ b/solution.py
@@ -126,20 +126,40 @@
     return (lax.rem(x + d[0] + GX, GX), lax.rem(y + d[1] + GY, GY), lax.rem(z + d[2] + GZ, GZ))
 
 
-PLANE = [(x, y, 0) for x in range(GX) for y in range(GY) if (x, y) != (0, 0)]
-LINE = [(0, 0, z) for z in range(1, GZ)]
-_norm = lambda d: (d[0] % GX, d[1] % GY, d[2] % GZ)
-PARTNERS = sorted({_norm(d) for d in DIRS + PLANE + LINE})
+_ring = lambda v, n: min(v, n - v)
+PLANE = sorted(
+    ((x, y) for x in range(GX) for y in range(GY)), key=lambda d: -_ring(d[0], GX) - _ring(d[1], GY)
+)
+
+
+def everyone(act):
+    x, y, z = here()
+    rows = [(lax.rem(x + d[0], GX), lax.rem(y + d[1], GY)) for d in PLANE]
+
+    def layer(i, carry):
+        up = lax.rem(i, 2)
+        there = lax.rem(z + 4 + (i // 2 + up) * (1 - 2 * up), GZ)
+        for r in rows:
+            act((r[0], r[1], there))
+        return carry
+
+    lax.fori_loop(0, GZ - 1, layer, 0)
+    for r in rows[:-1]:
+        act((r[0], r[1], z))
+
+
+def copy_to(src, dst, sems, k, device):
+    return pltpu.make_async_remote_copy(
+        src_ref=src, dst_ref=dst, send_sem=sems.at[2 * k], recv_sem=sems.at[2 * k + 1], device_id=device, device_id_type=MESH
+    )
 
 
 def remote(src, dst, sems, k, d):
-    return pltpu.make_async_remote_copy(
-        src_ref=src, dst_ref=dst, send_sem=sems.at[2 * k], recv_sem=sems.at[2 * k + 1], device_id=at(d), device_id_type=MESH
-    )
+    return copy_to(src, dst, sems, k, at(d))
 
 
 def exchange_start(send, recv, sems, k, faces):
-    for d in DIRS:
+    for d in reversed(DIRS):
         if (sum(map(abs, d)) == 1) == faces:
             o, n = OFFS[d]
             o2, _ = OFFS[tuple(-v for v in d)]
@@ -170,7 +190,7 @@
 
 
 def owner_start(send, recv, sems, k):
-    for c, o in enumerate(CORNERS):
+    for c, o in reversed(list(enumerate(CORNERS))):
         if c:
             remote(send.at[pl.ds(8 * c, 8)], recv.at[pl.ds(8 * c, 8)], sems, k, o).start()
 
@@ -183,49 +203,22 @@
     return out
 
 
-def gather_start(val, plane, sems, k):
-    x, y, _ = here()
-    ab = x * GY + y
-    odd = lax.rem(y, 2) == 1
-    plane[ab] = jnp.where(jnp.full((8, 128), odd), pltpu.roll(val, 4, 0), val)
-    for d in PLANE:
-        remote(plane.at[ab], plane.at[ab], sems, k, d).start()
-
-
-def gather_turn(plane, full, sems, k):
-    bulk_wait(plane.at[pl.ds(0, 15)], plane.at[pl.ds(0, 15)], sems, k)
-    _, _, z = here()
-    pos = place(z)
-    rows = [plane[2 * i] + plane[2 * i + 1] for i in range(8)]
-    mine = pl.ds(pl.multiple_of(pos * 64, 64), 64)
-    full[mine, :] = jnp.concatenate(rows, axis=0)
-    for d in LINE:
-        remote(full.at[mine], full.at[mine], sems, k + 1, d).start()
+def place(z):
+    h = z // 2
+    return lax.rem(z, 2) * h + (1 - lax.rem(z, 2)) * (6 - 2 * lax.rem(h, 2) + h // 2)
+
+
+def gather_start(val, full, sems, k):
+    x, y, z = here()
+    slot = place(z) * 16 + x * GY + y
+    full[slot] = val
+    everyone(lambda device: copy_to(full.at[slot], full.at[slot], sems, k, device).start())
 
 
 def gather_finish(full, sems, k):
-    bulk_wait(full.at[pl.ds(0, 448)], full.at[pl.ds(0, 448)], sems, k + 1)
-
-
-def reduce_start(val, plane, sems, k):
-    x, y, _ = here()
-    ab = x * GY + y
-    plane[ab] = val
-    for d in PLANE:
-        remote(plane.at[ab], plane.at[ab], sems, k, d).start()
-
-
-def reduce_turn(plane, line, sems, k):
-    bulk_wait(plane.at[pl.ds(0, 15)], plane.at[pl.ds(0, 15)], sems, k)
-    _, _, z = here()
-    line[z] = jnp.sum(plane[...], axis=0)
-    for d in LINE:
-        remote(line.at[z], line.at[z], sems, k + 1, d).start()
-
-
-def reduce_finish(line, sems, k):
-    bulk_wait(line.at[pl.ds(0, 7)], line.at[pl.ds(0, 7)], sems, k + 1)
-    return jnp.sum(line[...], axis=0)
+    rest = pl.ds(0, 127)
+    bulk_wait(full.at[rest], full.at[rest], sems, k)
+    return full[...]
 
 
 SPLIT = []
@@ -243,19 +236,13 @@
     return (lax.broadcasted_iota(jnp.int32, (ids.shape[0], n), 1) == ids).astype(F32).astype(BF16)
 
 
-def place(z):
-    h = z // 2
-    return lax.rem(z, 2) * h + (1 - lax.rem(z, 2)) * (6 - 2 * lax.rem(h, 2) + h // 2)
-
-
 def coords(m):
     pos = m >> 6
     c = jnp.where(pos < 4, 2 * pos + 1, jnp.where(pos < 6, 4 * pos - 14, 4 * pos - 24))
     return (m >> 4) & 3, (m >> 2) & 3, c, m & 3
 
 
-def build_coarse(kall_ref, kc):
-    kall = kall_ref[...]
+def build_coarse(kall, kc):
     ra, rb, rc, _ = coords(lax.broadcasted_iota(jnp.int32, (512, 128), 0))
     for j in range(4):
         ca, cb, cc, ct = coords(lax.broadcasted_iota(jnp.int32, (1, 128), 1) + 128 * j)
@@ -313,10 +300,9 @@
 def program(load_h, a_h, di_h, n_h, phi_h, bcol, icol, kcol, krow, wt_ref, s64_ref, tmask_ref, spread_ref,
             parts_ref,
             load_v, a_v, n_v, arows, nrows, di_v, phi_v, lb_v, li_v, send, recv, ssend, srecv,
-            ksend, krecv, hsend, hrecv, kplane, gplane, kfull, gfull, rplane, rline, kc, xo, x2, xf, sems, dsems):
+            ksend, krecv, hsend, hrecv, kfull, gfull, sums1, sums2, kc, xo, x2, xf, mark, sems, dsems):
     sem = pltpu.get_barrier_semaphore()
-    for d in PARTNERS:
-        pl.semaphore_signal(sem, inc=1, device_id=at(d), device_id_type=MESH)
+    everyone(lambda device: pl.semaphore_signal(sem, inc=1, device_id=device, device_id_type=MESH))
 
     get_phi = pltpu.make_async_copy(phi_h.at[:, 0, :], phi_v, dsems.at[0])
     get_load = pltpu.make_async_copy(load_h, load_v, dsems.at[1])
@@ -324,15 +310,22 @@
     get_phi.start()
     get_a = pltpu.make_async_copy(a_h.at[:, 0, :], a_v, dsems.at[3])
     get_n = pltpu.make_async_copy(n_h.at[:, 0, :], n_v, dsems.at[4])
-    get_a.start()
     get_load.start()
     get_di.start()
+    get_a.start()
     get_n.start()
 
     def border_rows(src, dst):
         dst[pl.ds(NB - 8, 8), :] = jnp.zeros((8, NODES), F32)
         for r, n, c in RUNS:
             dst[pl.ds(r, c), :] = src[pl.ds(n, c), :]
+
+    def fence():
+        def note(i, carry):
+            mark[i] = jnp.zeros((8, 128), F32)
+            return carry
+
+        lax.fori_loop(0, 2, note, 0)
 
     pb, pi, pk = choose(bcol, NODES), choose(icol, NODES), choose(kcol, NB)
     pkt = (lax.broadcasted_iota(jnp.int32, (NB, NS), 0) == krow[...]).astype(F32).astype(BF16)
@@ -343,14 +336,6 @@
     phi8 = jnp.concatenate([phi] * 8, axis=0)
     p24 = pick_cols(phi, pb)
     p64 = pick(s64_ref[...].astype(BF16), p24)
-    get_a.wait()
-    border_rows(a_v, arows)
-    ab = arows[...]
-    k64 = dot(p64, dot(ab, phi8, 1, 1)) * tmask_ref[...]
-    ksend[...] = pick_right(k64, spread_ref[...].astype(BF16))
-    pl.semaphore_wait(sem, len(PARTNERS))
-    owner_start(ksend, krecv, sems, 0)
-
     get_load.wait()
     lb_v[pl.ds(NB - 8, 8), :] = jnp.zeros((8, RHS), F32)
     for i, j, parts in SPLIT:
@@ -359,11 +344,21 @@
     lb, li = lb_v[...], li_v[...]
     get_di.wait()
     start = dot6(pieces(di_v[...]), li)
+    get_a.wait()
+    border_rows(a_v, arows)
+    ab = arows[...]
+    k64 = dot(p64, dot(ab, phi8, 1, 1)) * tmask_ref[...]
+    ksend[...] = pick_right(k64, spread_ref[...].astype(BF16))
+    pl.semaphore_wait(sem, GX * GY * GZ - 1)
+    owner_start(ksend, krecv, sems, 0)
+    fence()
+
     abi = pick_cols(ab, pi)
     c = lb - dot6(pieces(abi), start)
     cl = jnp.concatenate([c, lb], axis=1)
     swap_start(cl, pk, send, recv, sems, 18)
-    gather_start(owner_finish(ksend, krecv, sems, 0), kplane, sems, 2)
+    gather_start(owner_finish(ksend, krecv, sems, 0)[0:4], kfull, sems, 2)
+    fence()
     k0 = jnp.sum(li * start, axis=0, keepdims=True)
     p64 = pieces(p64)
     get_n.wait()
@@ -373,18 +368,16 @@
     f = wt * asm[:, 0:RHS]
     hsend[0] = dot6(p64, f)
     owner_start(hsend.at[0], hrecv.at[0], sems, 4)
-    gather_turn(kplane, kfull, sems, 2)
+    fence()
     w = dot6(nbb, f)
-    gather_start(owner_finish(hsend.at[0], hrecv.at[0], sems, 4), gplane.at[0], sems, 5)
-    gather_finish(kfull, sems, 2)
-
-    build_coarse(kfull, kc)
+    build_coarse(gather_finish(kfull, sems, 2).reshape(512, 128), kc)
     low = lax.broadcasted_iota(jnp.int32, (64, 128), 1) < 64
     for j in range(2):
         cut = pl.ds(128 * j, 128)
         xo[j] = jnp.where(low, kc[pl.ds(128 * j, 64), cut], kc[pl.ds(128 * j + 64, 64), cut])
     sweep(xo, 64)
-    gather_turn(gplane.at[0], gfull.at[0], sems, 5)
+    gather_start(owner_finish(hsend.at[0], hrecv.at[0], sems, 4)[0:4], gfull.at[0], sems, 5)
+    fence()
     group = lax.broadcasted_iota(jnp.int32, (64, 256), 1) // 64
     both = jnp.concatenate([xo[0], xo[1]], axis=1)
     inv_o = jnp.concatenate([jnp.where(group == g, both, 0.0) for g in range(4)], axis=0)
@@ -412,43 +405,60 @@
     we = jnp.concatenate([w2, wf], axis=1)
     w24 = jnp.concatenate([dot(so, inv_o) - dot(we, m, 1, 1), we], axis=1)
 
-    def apply_coarse(w, g):
-        return wt * (w + dot(p24, dot(w24, g), 0, 0))
+    def long(v, axis, order):
+        q = pieces(v)
+        return jnp.concatenate([q[i] for i in order], axis=axis)
+
+    p24t = wt[:, 0:1] * p24.T
+    spots = long(p24t, 1, (0, 0, 0, 1, 1, 2))
+    packed = mm(pk, spots).astype(BF16)
+
+    def correct_start(w, wpk, g, send, recv, k):
+        y = long(dot(w24, g), 0, (0, 1, 2, 0, 1, 0))
+        send[REST_ROWS, :] = wpk[NF:] + mm(packed[NF:], y)
+        exchange_start(send, recv, sems, k + 1, False)
+        send[FACE_ROWS, :] = wpk[:NF] + mm(packed[:NF], y)
+        exchange_start(send, recv, sems, k, True)
+        return w + mm(spots, y)
 
     part = lambda a, b: jnp.sum(a * b, axis=0, keepdims=True)
-    gather_finish(gfull.at[0], sems, 5)
-    u = apply_coarse(w, gfull[0])
-    swap_start(u, pk, ssend.at[0], srecv.at[0], sems, 20)
+    w = wt * w
+    wpk = pick(pk, w)
+    g = gather_finish(gfull.at[0], sems, 5).reshape(512, RHS)
+    u = correct_start(w, wpk, g, ssend.at[0], srecv.at[0], 20)
+    fence()
     x = dot(di_v[...], abi, 1, 1)
     s = pieces(pick_cols(ab, pb) - dot(abi, x))
     z1 = swap_finish(u, pkt, ssend.at[0], srecv.at[0], sems, 20)
     t1 = dot6(s, z1)
     swap_start(t1, pk, ssend.at[1], srecv.at[1], sems, 22)
-    reduce_start(jnp.concatenate([k0, part(c, z1), part(z1, t1), jnp.zeros((5, RHS), F32)], axis=0), rplane.at[0], sems, 11)
+    fence()
+    gather_start(jnp.concatenate([k0, part(c, z1), part(z1, t1), jnp.zeros((1, RHS), F32)], axis=0), sums1, sems, 11)
     at1 = swap_finish(t1, pkt, ssend.at[1], srecv.at[1], sems, 22)
     f = wt * at1
     hsend[1] = dot6(p64, f)
     owner_start(hsend.at[1], hrecv.at[1], sems, 13)
-    w = dot6(nbb, f)
-    reduce_turn(rplane.at[0], rline.at[0], sems, 11)
-    gather_start(owner_finish(hsend.at[1], hrecv.at[1], sems, 13), gplane.at[1], sems, 14)
-    gather_turn(gplane.at[1], gfull.at[1], sems, 14)
-    sums = reduce_finish(rline.at[0], sems, 11)
+    fence()
+    w = wt * dot6(nbb, f)
+    wpk = pick(pk, w)
+    gather_start(owner_finish(hsend.at[1], hrecv.at[1], sems, 13)[0:4], gfull.at[1], sems, 14)
+    fence()
+    sums = jnp.sum(gather_finish(sums1, sems, 11), axis=0)
     k0s = sums[0:1]
     g0 = k0s + sums[1:2]
     s1 = g0 / (k0s + sums[2:3])
-    gather_finish(gfull.at[1], sems, 14)
-    u = apply_coarse(w, gfull[1])
-    swap_start(u, pk, ssend.at[2], srecv.at[2], sems, 24)
+    g = gather_finish(gfull.at[1], sems, 14).reshape(512, RHS)
+    u = correct_start(w, wpk, g, ssend.at[2], srecv.at[2], 24)
     z2 = swap_finish(u, pkt, ssend.at[2], srecv.at[2], sems, 24)
     t2 = dot6(s, z2)
     swap_start(t2, pk, ssend.at[3], srecv.at[3], sems, 26)
+    fence()
     zp, tp, cp = z1 - s1 * z2, t1 - s1 * t2, c - s1 * t1
-    reduce_start(jnp.concatenate([part(cp, zp), part(zp, tp), jnp.zeros((6, RHS), F32)], axis=0), rplane.at[1], sems, 16)
+    gather_start(jnp.concatenate([part(cp, zp), part(zp, tp)], axis=0), sums2, sems, 16)
+    fence()
     xz = dot(x, jnp.concatenate([z1, zp], axis=1))
     at2 = swap_finish(t2, pkt, ssend.at[3], srecv.at[3], sems, 26)
-    reduce_turn(rplane.at[1], rline.at[1], sems, 16)
-    last = reduce_finish(rline.at[1], sems, 16)
+    last = jnp.sum(gather_finish(sums2, sems, 16), axis=0)
     rest = 1.0 - s1
     g1 = rest * rest * k0s + last[0:1]
     beta = g1 / g0
@@ -487,8 +497,8 @@
         scratch_shapes=[
             V(M, M, M, RHS), V(NODES, NODES), V(NODES, NODES), V(NB, NODES), V(NB, NODES), V(NI, NI), V(20, NODES), V(NB, RHS), V(NI, RHS),
             V(NS, 2 * RHS), V(NS, 2 * RHS), V(4, NS, RHS), V(4, NS, RHS),
-            V(64, 128), V(64, 128), V(2, 64, 128), V(2, 64, 128), V(16, 8, 128), V(2, 16, 8, 128), V(512, 128), V(2, 512, 128),
-            V(2, 16, 8, 128), V(2, 8, 8, 128), V(512, 512), V(2, 64, 128), V(1, 64, 128), V(1, 128, 128),
+            V(64, 128), V(64, 128), V(2, 64, 128), V(2, 64, 128), V(128, 4, 128), V(2, 128, 4, 128),
+            V(128, 4, 128), V(128, 2, 128), V(512, 512), V(2, 64, 128), V(1, 64, 128), V(1, 128, 128), V(2, 8, 128),
             pltpu.SemaphoreType.DMA((56,)), pltpu.SemaphoreType.DMA((5,)),
         ],
         compiler_params=pltpu.CompilerParams(vmem_limit_bytes=60 * 2**20, collective_id=0, has_side_effects=True),

time: 96.6 us -> 89.6 us (0.928)
  Pallas kernels: 94.7 us -> 87.6 us
    pallas_call x1, Pallas kernels: 93.5 us -> 86.4 us  [local(): pl.pallas_call(program, out_shape=jax.ShapeDtypeStruct((2 * NB + 688, RHS...]
where the time goes in v2:
time: 89.6 us; the launch traced here: 89.4 us
  Pallas kernels  87.6 us (98%)
  local copies, waits for them, and re-layouts  1.11 us (1%)
    pallas_call x1, Pallas kernels, local(): pl.pallas_call(program, out_shape=jax.ShapeDtypeStruct((2 * NB + 688, RHS...  86.4 us

profile of v2, /device:TPU:1, one launch (start us, length us, event | category | flops | bytes accessed | tf_op | source)
XLA Modules:
  0.0 89.4 jit_solution(3936207216966038288)
XLA Ops:
  0.6 86.4 %program.1.parts_ref = f32[1472,128]{1,0:T(8,128)} custom-call(f32[9,9,9,128]{3,2,1,0:T(8,128)} %load_h.1, f32[729,1,729]{2,1,0:T(1,128)} %bitcast.4, f32[343,1,343]{2,1,0:T(1,128)} %bitcast.6, f32[729,1,729]{2,1,0:T(1,128)} %bitcast.5, f32[20,1,729]{2,1,0:T(1,128)} %bitcast.7, s32[392,1]{1,0:T(8,128)} %constant.16.clone.bcol, ...), custom_call_target="tpu_custom_call" | custom-call | tf_op jit(solution)/shard_map/program/pallas_call | solution.py:492
  87.1 0.0 copy-start
  87.1 1.1 %copy-done = f32[1472,128]{1,0:T(8,128)S(1)} copy-done((f32[1472,128]{1,0:T(8,128)S(1)}, f32[1472,128]{1,0:T(8,128)}, u32[]{:S(2)}) %copy-start) | copy-done | bytes 753688
  88.2 1.2 %spread.1 = (f32[9,9,9,128]{3,2,1,0:T(8,128)}, f32[9,9,9,128]{3,2,1,0:T(8,128)}) custom-call(f32[1472,128]{1,0:T(8,128)S(1)} %copy-done), custom_call_target="tpu_custom_call" | custom-call | tf_op jit(solution)/shard_map/spread/pallas_call | solution.py:507
Async XLA Ops:
  87.1 1.1 %copy-start = (f32[1472,128]{1,0:T(8,128)S(1)}, f32[1472,128]{1,0:T(8,128)}, u32[]{:S(2)}) copy-start(f32[1472,128]{1,0:T(8,128)} %program.1.parts_ref) | copy-start | bytes 2260996

commit v3 on v2

--- a/solution.py
+++ b/solution.py
@@ -301,8 +301,6 @@
             parts_ref,
             load_v, a_v, n_v, arows, nrows, di_v, phi_v, lb_v, li_v, send, recv, ssend, srecv,
             ksend, krecv, hsend, hrecv, kfull, gfull, sums1, sums2, kc, xo, x2, xf, mark, sems, dsems):
-    sem = pltpu.get_barrier_semaphore()
-    everyone(lambda device: pl.semaphore_signal(sem, inc=1, device_id=device, device_id_type=MESH))
 
     get_phi = pltpu.make_async_copy(phi_h.at[:, 0, :], phi_v, dsems.at[0])
     get_load = pltpu.make_async_copy(load_h, load_v, dsems.at[1])
@@ -314,6 +312,8 @@
     get_di.start()
     get_a.start()
     get_n.start()
+    sem = pltpu.get_barrier_semaphore()
+    everyone(lambda device: pl.semaphore_signal(sem, inc=1, device_id=device, device_id_type=MESH))
 
     def border_rows(src, dst):
         dst[pl.ds(NB - 8, 8), :] = jnp.zeros((8, NODES), F32)
@@ -355,8 +355,7 @@
 
     abi = pick_cols(ab, pi)
     c = lb - dot6(pieces(abi), start)
-    cl = jnp.concatenate([c, lb], axis=1)
-    swap_start(cl, pk, send, recv, sems, 18)
+    swap_start(c, pk, send.at[0], recv.at[0], sems, 18)
     gather_start(owner_finish(ksend, krecv, sems, 0)[0:4], kfull, sems, 2)
     fence()
     k0 = jnp.sum(li * start, axis=0, keepdims=True)
@@ -364,12 +363,13 @@
     get_n.wait()
     border_rows(n_v, nrows)
     nbb = pieces(pick_cols(nrows[...], pb))
-    asm = swap_finish(cl, pkt, send, recv, sems, 18)
-    f = wt * asm[:, 0:RHS]
+    ac = swap_finish(c, pkt, send.at[0], recv.at[0], sems, 18)
+    f = wt * ac
     hsend[0] = dot6(p64, f)
     owner_start(hsend.at[0], hrecv.at[0], sems, 4)
     fence()
-    w = dot6(nbb, f)
+    w = wt * dot6(nbb, f)
+    wpk = pick(pk, w)
     build_coarse(gather_finish(kfull, sems, 2).reshape(512, 128), kc)
     low = lax.broadcasted_iota(jnp.int32, (64, 128), 1) < 64
     for j in range(2):
@@ -422,8 +422,6 @@
         return w + mm(spots, y)
 
     part = lambda a, b: jnp.sum(a * b, axis=0, keepdims=True)
-    w = wt * w
-    wpk = pick(pk, w)
     g = gather_finish(gfull.at[0], sems, 5).reshape(512, RHS)
     u = correct_start(w, wpk, g, ssend.at[0], srecv.at[0], 20)
     fence()
@@ -443,6 +441,7 @@
     wpk = pick(pk, w)
     gather_start(owner_finish(hsend.at[1], hrecv.at[1], sems, 13)[0:4], gfull.at[1], sems, 14)
     fence()
+    swap_start(lb, pk, send.at[1], recv.at[1], sems, 28)
     sums = jnp.sum(gather_finish(sums1, sems, 11), axis=0)
     k0s = sums[0:1]
     g0 = k0s + sums[1:2]
@@ -451,11 +450,12 @@
     u = correct_start(w, wpk, g, ssend.at[2], srecv.at[2], 24)
     z2 = swap_finish(u, pkt, ssend.at[2], srecv.at[2], sems, 24)
     t2 = dot6(s, z2)
-    swap_start(t2, pk, ssend.at[3], srecv.at[3], sems, 26)
-    fence()
     zp, tp, cp = z1 - s1 * z2, t1 - s1 * t2, c - s1 * t1
     gather_start(jnp.concatenate([part(cp, zp), part(zp, tp)], axis=0), sums2, sems, 16)
     fence()
+    swap_start(t2, pk, ssend.at[3], srecv.at[3], sems, 26)
+    fence()
+    al = swap_finish(lb, pkt, send.at[1], recv.at[1], sems, 28)
     xz = dot(x, jnp.concatenate([z1, zp], axis=1))
     at2 = swap_finish(t2, pkt, ssend.at[3], srecv.at[3], sems, 26)
     last = jnp.sum(gather_finish(sums2, sems, 16), axis=0)
@@ -467,8 +467,7 @@
     xb = s1 * z1 + s2 * (zp + beta * z1)
     xi = (s1 + s2 * (rest + beta)) * start - (s1 + s2 * beta) * xz[:, :RHS] - s2 * xz[:, RHS:]
     kappa = rest * (1.0 - s2) - s2 * beta
-    ac = asm[:, 0:RHS]
-    ae = asm[:, RHS : 2 * RHS] - ac
+    ae = al - ac
     rb = kappa * ae + (ac - s1 * at1) - s2 * ((at1 - s1 * at2) + beta * at1)
     parts_ref[pl.ds(AT[0], NB), :], parts_ref[pl.ds(AT[1], NI), :] = xb, xi
     parts_ref[pl.ds(AT[2], NB), :], parts_ref[pl.ds(AT[3], NI), :] = rb, kappa * li
@@ -496,10 +495,10 @@
         out_specs=VM,
         scratch_shapes=[
             V(M, M, M, RHS), V(NODES, NODES), V(NODES, NODES), V(NB, NODES), V(NB, NODES), V(NI, NI), V(20, NODES), V(NB, RHS), V(NI, RHS),
-            V(NS, 2 * RHS), V(NS, 2 * RHS), V(4, NS, RHS), V(4, NS, RHS),
+            V(2, NS, RHS), V(2, NS, RHS), V(4, NS, RHS), V(4, NS, RHS),
             V(64, 128), V(64, 128), V(2, 64, 128), V(2, 64, 128), V(128, 4, 128), V(2, 128, 4, 128),
             V(128, 4, 128), V(128, 2, 128), V(512, 512), V(2, 64, 128), V(1, 64, 128), V(1, 128, 128), V(2, 8, 128),
-            pltpu.SemaphoreType.DMA((56,)), pltpu.SemaphoreType.DMA((5,)),
+            pltpu.SemaphoreType.DMA((60,)), pltpu.SemaphoreType.DMA((5,)),
         ],
         compiler_params=pltpu.CompilerParams(vmem_limit_bytes=60 * 2**20, collective_id=0, has_side_effects=True),
         name="program",

time: 89.6 us -> 85.3 us (0.952)
  Pallas kernels: 87.6 us -> 83.1 us
    pallas_call x1, Pallas kernels: 86.4 us -> 81.9 us  [local(): pl.pallas_call(program, out_shape=jax.ShapeDtypeStruct((2 * NB + 688, RHS...]
where the time goes in v3:
time: 85.3 us; the launch traced here: 84.9 us
  Pallas kernels  83.1 us (97%)
  local copies, waits for them, and re-layouts  1.11 us (1%)
    pallas_call x1, Pallas kernels, local(): pl.pallas_call(program, out_shape=jax.ShapeDtypeStruct((2 * NB + 688, RHS...  81.9 us

profile of v3, /device:TPU:1, one launch (start us, length us, event | category | flops | bytes accessed | tf_op | source)
XLA Modules:
  0.0 84.9 jit_solution(3944843890216624543)
XLA Ops:
  0.6 81.9 %program.1.parts_ref = f32[1472,128]{1,0:T(8,128)} custom-call(f32[9,9,9,128]{3,2,1,0:T(8,128)} %load_h.1, f32[729,1,729]{2,1,0:T(1,128)} %bitcast.4, f32[343,1,343]{2,1,0:T(1,128)} %bitcast.6, f32[729,1,729]{2,1,0:T(1,128)} %bitcast.5, f32[20,1,729]{2,1,0:T(1,128)} %bitcast.7, s32[392,1]{1,0:T(8,128)} %constant.16.clone.bcol, ...), custom_call_target="tpu_custom_call" | custom-call | tf_op jit(solution)/shard_map/program/pallas_call | solution.py:491
  82.5 0.0 copy-start
  82.5 1.1 %copy-done = f32[1472,128]{1,0:T(8,128)S(1)} copy-done((f32[1472,128]{1,0:T(8,128)S(1)}, f32[1472,128]{1,0:T(8,128)}, u32[]{:S(2)}) %copy-start) | copy-done | bytes 753688
  83.7 1.2 %spread.1 = (f32[9,9,9,128]{3,2,1,0:T(8,128)}, f32[9,9,9,128]{3,2,1,0:T(8,128)}) custom-call(f32[1472,128]{1,0:T(8,128)S(1)} %copy-done), custom_call_target="tpu_custom_call" | custom-call | tf_op jit(solution)/shard_map/spread/pallas_call | solution.py:506
Async XLA Ops:
  82.5 1.1 %copy-start = (f32[1472,128]{1,0:T(8,128)S(1)}, f32[1472,128]{1,0:T(8,128)}, u32[]{:S(2)}) copy-start(f32[1472,128]{1,0:T(8,128)} %program.1.parts_ref) | copy-start | bytes 2260996

commit v4 on v3

--- a/solution.py
+++ b/solution.py
@@ -31,7 +31,13 @@
 
 B_COL = np.full((NB, 1), -1, np.int32)
 B_COL[: len(B_IDS), 0] = B_IDS
-I_COL = I_IDS.astype(np.int32)[:, None]
+NEAR_NODE = np.full((NB, 1), -1, np.int32)
+NEAR = np.full((NB, 1), -1, np.int32)
+for _r, _n in enumerate(B_IDS):
+    if _rim[_n] == 1:
+        _i, _j, _k = (min(max(int(v), 1), M - 2) for v in (_n // 81, _n // 9 % 9, _n % 9))
+        NEAR_NODE[_r, 0] = (_i * M + _j) * M + _k
+        NEAR[_r, 0] = I_POS[(_i * M + _j) * M + _k]
 RUNS, _r = [], 0
 while _r < len(B_IDS):
     _e = _r + 1
@@ -297,7 +303,7 @@
     lax.fori_loop(0, n // 4, body, 0)
 
 
-def program(load_h, a_h, di_h, n_h, phi_h, bcol, icol, kcol, krow, wt_ref, s64_ref, tmask_ref, spread_ref,
+def program(load_h, a_h, di_h, n_h, phi_h, bcol, nearnode, nearcol, kcol, krow, wt_ref, s64_ref, tmask_ref, spread_ref,
             parts_ref,
             load_v, a_v, n_v, arows, nrows, di_v, phi_v, lb_v, li_v, send, recv, ssend, srecv,
             ksend, krecv, hsend, hrecv, kfull, gfull, sums1, sums2, kc, xo, x2, xf, mark, sems, dsems):
@@ -327,7 +333,7 @@
 
         lax.fori_loop(0, 2, note, 0)
 
-    pb, pi, pk = choose(bcol, NODES), choose(icol, NODES), choose(kcol, NB)
+    pb, near, pk = choose(bcol, NODES), choose(nearcol, NI), choose(kcol, NB)
     pkt = (lax.broadcasted_iota(jnp.int32, (NB, NS), 0) == krow[...]).astype(F32).astype(BF16)
     wt = wt_ref[...]
 
@@ -353,8 +359,9 @@
     owner_start(ksend, krecv, sems, 0)
     fence()
 
-    abi = pick_cols(ab, pi)
-    c = lb - dot6(pieces(abi), start)
+    spot = lax.broadcasted_iota(jnp.int32, (NB, NODES), 1) == nearnode[...]
+    tie = jnp.sum(jnp.where(spot, ab, 0.0), axis=1, keepdims=True)
+    c = lb - tie * pick(near, start)
     swap_start(c, pk, send.at[0], recv.at[0], sems, 18)
     gather_start(owner_finish(ksend, krecv, sems, 0)[0:4], kfull, sems, 2)
     fence()
@@ -425,8 +432,8 @@
     g = gather_finish(gfull.at[0], sems, 5).reshape(512, RHS)
     u = correct_start(w, wpk, g, ssend.at[0], srecv.at[0], 20)
     fence()
-    x = dot(di_v[...], abi, 1, 1)
-    s = pieces(pick_cols(ab, pb) - dot(abi, x))
+    x = pick_cols(di_v[...], near) * jnp.broadcast_to(tie, (NB, 128)).T[0:1, :]
+    s = pieces(pick_cols(ab, pb) - tie * pick(near, x))
     z1 = swap_finish(u, pkt, ssend.at[0], srecv.at[0], sems, 20)
     t1 = dot6(s, z1)
     swap_start(t1, pk, ssend.at[1], srecv.at[1], sems, 22)
@@ -456,7 +463,9 @@
     swap_start(t2, pk, ssend.at[3], srecv.at[3], sems, 26)
     fence()
     al = swap_finish(lb, pkt, send.at[1], recv.at[1], sems, 28)
-    xz = dot(x, jnp.concatenate([z1, zp], axis=1))
+    x1, x2_, _ = pieces(x)
+    both1, both2, _ = pieces(jnp.concatenate([z1, zp], axis=1))
+    xz = mm(x1, both1) + (mm(x1, both2) + mm(x2_, both1))
     at2 = swap_finish(t2, pkt, ssend.at[3], srecv.at[3], sems, 26)
     last = jnp.sum(gather_finish(sums2, sems, 16), axis=0)
     rest = 1.0 - s1
@@ -485,7 +494,7 @@
 
 
 def local(load, a, di, n, phi):
-    tables = [jnp.asarray(v) for v in (B_COL, I_COL, K_COL, K_COL.T, WEIGHT, S64, TMASK, SPREAD)]
+    tables = [jnp.asarray(v) for v in (B_COL, NEAR_NODE, NEAR, K_COL, K_COL.T, WEIGHT, S64, TMASK, SPREAD)]
     V = lambda *s: pltpu.VMEM(s, F32)
     shape = jax.ShapeDtypeStruct((M, M, M, RHS), F32)
     parts = pl.pallas_call(

time: 85.3 us -> 83.9 us (0.984)
  Pallas kernels: 83.1 us -> 82 us
    pallas_call x1, Pallas kernels: 81.9 us -> 80.8 us  [local(): pl.pallas_call(program, out_shape=jax.ShapeDtypeStruct((2 * NB + 688, RHS...]
where the time goes in v4:
time: 83.9 us; the launch traced here: 83.8 us
  Pallas kernels  82 us (98%)
  local copies, waits for them, and re-layouts  1.11 us (1%)
    pallas_call x1, Pallas kernels, local(): pl.pallas_call(program, out_shape=jax.ShapeDtypeStruct((2 * NB + 688, RHS...  80.8 us

profile of v4, /device:TPU:1, one launch (start us, length us, event | category | flops | bytes accessed | tf_op | source)
XLA Modules:
  0.0 83.8 jit_solution(2281100857284210144)
XLA Ops:
  0.6 80.8 %program.1.parts_ref = f32[1472,128]{1,0:T(8,128)} custom-call(f32[9,9,9,128]{3,2,1,0:T(8,128)} %load_h.1, f32[729,1,729]{2,1,0:T(1,128)} %bitcast.4, f32[343,1,343]{2,1,0:T(1,128)} %bitcast.6, f32[729,1,729]{2,1,0:T(1,128)} %bitcast.5, f32[20,1,729]{2,1,0:T(1,128)} %bitcast.7, s32[392,1]{1,0:T(8,128)} %constant.18.clone.bcol, ...), custom_call_target="tpu_custom_call" | custom-call | tf_op jit(solution)/shard_map/program/pallas_call | solution.py:500
  81.4 0.0 copy-start
  81.4 1.1 %copy-done = f32[1472,128]{1,0:T(8,128)S(1)} copy-done((f32[1472,128]{1,0:T(8,128)S(1)}, f32[1472,128]{1,0:T(8,128)}, u32[]{:S(2)}) %copy-start) | copy-done | bytes 753688
  82.6 1.2 %spread.1 = (f32[9,9,9,128]{3,2,1,0:T(8,128)}, f32[9,9,9,128]{3,2,1,0:T(8,128)}) custom-call(f32[1472,128]{1,0:T(8,128)S(1)} %copy-done), custom_call_target="tpu_custom_call" | custom-call | tf_op jit(solution)/shard_map/spread/pallas_call | solution.py:515
Async XLA Ops:
  81.4 1.1 %copy-start = (f32[1472,128]{1,0:T(8,128)S(1)}, f32[1472,128]{1,0:T(8,128)}, u32[]{:S(2)}) copy-start(f32[1472,128]{1,0:T(8,128)} %program.1.parts_ref) | copy-start | bytes 2260996

commit v5 on v4

--- a/solution.py
+++ b/solution.py
@@ -276,15 +276,17 @@
             e, f, g, h = take(rows[0], top[2]), take(rows[0], top[3]), take(rows[1], top[2]), take(rows[1], top[3])
             p, q, r = take(rows[2], top[2]), take(rows[2], top[3]), take(rows[3], top[3])
             cols = [take(x, v) for v in idx]
-            d = 1.0 / (a * c - b * b)
-            a, b, c = c * d, -b * d, a * d
-            we, wf, wg, wh = a * e + b * g, a * f + b * h, b * e + c * g, b * f + c * h
-            p, q, r = p - (e * we + g * wg), q - (e * wf + g * wh), r - (f * wf + h * wh)
-            d = 1.0 / (p * r - q * q)
-            p, q, r = r * d, -q * d, p * d
-            ue, uf, ug, uh = we * p + wf * q, we * q + wf * r, wg * p + wh * q, wg * q + wh * r
-            a, b, c = a + (ue * we + uf * wf), b + (ue * wg + uf * wh), c + (ug * wg + uh * wh)
-            inv = [[a, b, -ue, -uf], [b, c, -ug, -uh], [-ue, -ug, p, q], [-uf, -uh, q, r]]
+            s0, s1, s2 = a * c - b * b, a * g - b * e, a * h - b * f
+            s3, s4, s5 = b * g - c * e, b * h - c * f, e * h - g * f
+            c5, c4, c3 = p * r - q * q, g * r - h * q, g * q - h * p
+            c2, c1, c0 = e * r - f * q, e * q - f * p, e * h - f * g
+            d = 1.0 / (((s0 * c5 - s1 * c4) + (s2 * c3 + s3 * c2)) + (s5 * c0 - s4 * c1))
+            i00, i01 = (c * c5 - g * c4 + h * c3) * d, (e * c4 - b * c5 - f * c3) * d
+            i02, i03 = (h * s5 - q * s4 + r * s3) * d, (p * s4 - g * s5 - q * s3) * d
+            i11, i12 = (a * c5 - e * c2 + f * c1) * d, (q * s2 - f * s5 - r * s1) * d
+            i13, i22 = (e * s5 - p * s2 + q * s1) * d, (f * s4 - h * s2 + r * s0) * d
+            i23, i33 = (g * s2 - e * s4 - q * s0) * d, (e * s3 - g * s1 + p * s0) * d
+            inv = [[i00, i01, i02, i03], [i01, i11, i12, i13], [i02, i12, i22, i23], [i03, i13, i23, i33]]
             on = [lane[0:8] == v for v in top]
             new = []
             for m in inv:
@@ -377,6 +379,7 @@
     fence()
     w = wt * dot6(nbb, f)
     wpk = pick(pk, w)
+    swap_start(lb, pk, send.at[1], recv.at[1], sems, 28)
     build_coarse(gather_finish(kfull, sems, 2).reshape(512, 128), kc)
     low = lax.broadcasted_iota(jnp.int32, (64, 128), 1) < 64
     for j in range(2):
@@ -397,7 +400,6 @@
     k2f = se[0:128, 128:256]
     m2 = dot(inv_2, k2f)
     xf[0] = se[128:256, 128:256] - dot(k2f, m2, 0, 0)
-    sweep(xf, 128)
     prim = lax.broadcasted_iota(jnp.int32, (24, 512), 0)
     want = jnp.full((24, 512), -1, jnp.int32)
     for q, (t, o) in enumerate(PRIM):
@@ -407,10 +409,11 @@
     so = sel[:, 0:256]
     s_e = sel[:, 256:512] - dot(so, m)
     s_2 = s_e[:, 0:128]
-    wf = dot(s_e[:, 128:256] - dot(s_2, m2), xf[0])
-    w2 = dot(s_2, inv_2) - dot(wf, m2, 1, 1)
-    we = jnp.concatenate([w2, wf], axis=1)
-    w24 = jnp.concatenate([dot(so, inv_o) - dot(we, m, 1, 1), we], axis=1)
+    s_f, from_2, from_o = s_e[:, 128:256] - dot(s_2, m2), dot(s_2, inv_2), dot(so, inv_o)
+    sweep(xf, 128)
+    wf = dot(s_f, xf[0])
+    we = jnp.concatenate([from_2 - dot(wf, m2, 1, 1), wf], axis=1)
+    w24 = jnp.concatenate([from_o - dot(we, m, 1, 1), we], axis=1)
 
     def long(v, axis, order):
         q = pieces(v)
@@ -448,7 +451,6 @@
     wpk = pick(pk, w)
     gather_start(owner_finish(hsend.at[1], hrecv.at[1], sems, 13)[0:4], gfull.at[1], sems, 14)
     fence()
-    swap_start(lb, pk, send.at[1], recv.at[1], sems, 28)
     sums = jnp.sum(gather_finish(sums1, sems, 11), axis=0)
     k0s = sums[0:1]
     g0 = k0s + sums[1:2]

time: 83.9 us -> 83.7 us (level)
  no operation moved by 1% of the time
where the time goes in v5:
time: 83.7 us; the launch traced here: 83.5 us
  Pallas kernels  81.7 us (98%)
  local copies, waits for them, and re-layouts  1.11 us (1%)
    pallas_call x1, Pallas kernels, local(): pl.pallas_call(program, out_shape=jax.ShapeDtypeStruct((2 * NB + 688, RHS...  80.5 us

profile of v5, /device:TPU:1, one launch (start us, length us, event | category | flops | bytes accessed | tf_op | source)
XLA Modules:
  0.0 83.5 jit_solution(16995056029712271624)
XLA Ops:
  0.6 80.5 %program.1.parts_ref = f32[1472,128]{1,0:T(8,128)} custom-call(f32[9,9,9,128]{3,2,1,0:T(8,128)} %load_h.1, f32[729,1,729]{2,1,0:T(1,128)} %bitcast.4, f32[343,1,343]{2,1,0:T(1,128)} %bitcast.6, f32[729,1,729]{2,1,0:T(1,128)} %bitcast.5, f32[20,1,729]{2,1,0:T(1,128)} %bitcast.7, s32[392,1]{1,0:T(8,128)} %constant.18.clone.bcol, ...), custom_call_target="tpu_custom_call" | custom-call | tf_op jit(solution)/shard_map/program/pallas_call | solution.py:502
  81.2 0.0 copy-start
  81.2 1.1 %copy-done = f32[1472,128]{1,0:T(8,128)S(1)} copy-done((f32[1472,128]{1,0:T(8,128)S(1)}, f32[1472,128]{1,0:T(8,128)}, u32[]{:S(2)}) %copy-start) | copy-done | bytes 753688
  82.3 1.2 %spread.1 = (f32[9,9,9,128]{3,2,1,0:T(8,128)}, f32[9,9,9,128]{3,2,1,0:T(8,128)}) custom-call(f32[1472,128]{1,0:T(8,128)S(1)} %copy-done), custom_call_target="tpu_custom_call" | custom-call | tf_op jit(solution)/shard_map/spread/pallas_call | solution.py:517
Async XLA Ops:
  81.2 1.1 %copy-start = (f32[1472,128]{1,0:T(8,128)S(1)}, f32[1472,128]{1,0:T(8,128)}, u32[]{:S(2)}) copy-start(f32[1472,128]{1,0:T(8,128)} %program.1.parts_ref) | copy-start | bytes 2260996

commit v6 on v4

--- a/solution.py
+++ b/solution.py
@@ -333,8 +333,7 @@
 
         lax.fori_loop(0, 2, note, 0)
 
-    pb, near, pk = choose(bcol, NODES), choose(nearcol, NI), choose(kcol, NB)
-    pkt = (lax.broadcasted_iota(jnp.int32, (NB, NS), 0) == krow[...]).astype(F32).astype(BF16)
+    pb = choose(bcol, NODES)
     wt = wt_ref[...]
 
     get_phi.wait()
@@ -358,6 +357,8 @@
     pl.semaphore_wait(sem, GX * GY * GZ - 1)
     owner_start(ksend, krecv, sems, 0)
     fence()
+    near, pk = choose(nearcol, NI), choose(kcol, NB)
+    pkt = (lax.broadcasted_iota(jnp.int32, (NB, NS), 0) == krow[...]).astype(F32).astype(BF16)
 
     spot = lax.broadcasted_iota(jnp.int32, (NB, NODES), 1) == nearnode[...]
     tie = jnp.sum(jnp.where(spot, ab, 0.0), axis=1, keepdims=True)
@@ -397,7 +398,6 @@
     k2f = se[0:128, 128:256]
     m2 = dot(inv_2, k2f)
     xf[0] = se[128:256, 128:256] - dot(k2f, m2, 0, 0)
-    sweep(xf, 128)
     prim = lax.broadcasted_iota(jnp.int32, (24, 512), 0)
     want = jnp.full((24, 512), -1, jnp.int32)
     for q, (t, o) in enumerate(PRIM):
@@ -407,10 +407,11 @@
     so = sel[:, 0:256]
     s_e = sel[:, 256:512] - dot(so, m)
     s_2 = s_e[:, 0:128]
-    wf = dot(s_e[:, 128:256] - dot(s_2, m2), xf[0])
-    w2 = dot(s_2, inv_2) - dot(wf, m2, 1, 1)
-    we = jnp.concatenate([w2, wf], axis=1)
-    w24 = jnp.concatenate([dot(so, inv_o) - dot(we, m, 1, 1), we], axis=1)
+    s_f, from_2, from_o = s_e[:, 128:256] - dot(s_2, m2), dot(s_2, inv_2), dot(so, inv_o)
+    sweep(xf, 128)
+    wf = dot(s_f, xf[0])
+    we = jnp.concatenate([from_2 - dot(wf, m2, 1, 1), wf], axis=1)
+    w24 = jnp.concatenate([from_o - dot(we, m, 1, 1), we], axis=1)
 
     def long(v, axis, order):
         q = pieces(v)

time: 83.9 us -> 83.2 us (level)
  no operation moved by 1% of the time
where the time goes in v6:
time: 83.2 us; the launch traced here: 83 us
  Pallas kernels  81.2 us (98%)
  local copies, waits for them, and re-layouts  1.11 us (1%)
    pallas_call x1, Pallas kernels, local(): pl.pallas_call(program, out_shape=jax.ShapeDtypeStruct((2 * NB + 688, RHS...  80 us

profile of v6, /device:TPU:1, one launch (start us, length us, event | category | flops | bytes accessed | tf_op | source)
XLA Modules:
  0.0 83.0 jit_solution(12855652377925394932)
XLA Ops:
  0.6 80.0 %program.1.parts_ref = f32[1472,128]{1,0:T(8,128)} custom-call(f32[9,9,9,128]{3,2,1,0:T(8,128)} %load_h.1, f32[729,1,729]{2,1,0:T(1,128)} %bitcast.4, f32[343,1,343]{2,1,0:T(1,128)} %bitcast.6, f32[729,1,729]{2,1,0:T(1,128)} %bitcast.5, f32[20,1,729]{2,1,0:T(1,128)} %bitcast.7, s32[392,1]{1,0:T(8,128)} %constant.18.clone.bcol, ...), custom_call_target="tpu_custom_call" | custom-call | tf_op jit(solution)/shard_map/program/pallas_call | solution.py:501
  80.7 0.0 copy-start
  80.7 1.1 %copy-done = f32[1472,128]{1,0:T(8,128)S(1)} copy-done((f32[1472,128]{1,0:T(8,128)S(1)}, f32[1472,128]{1,0:T(8,128)}, u32[]{:S(2)}) %copy-start) | copy-done | bytes 753688
  81.8 1.2 %spread.1 = (f32[9,9,9,128]{3,2,1,0:T(8,128)}, f32[9,9,9,128]{3,2,1,0:T(8,128)}) custom-call(f32[1472,128]{1,0:T(8,128)S(1)} %copy-done), custom_call_target="tpu_custom_call" | custom-call | tf_op jit(solution)/shard_map/spread/pallas_call | solution.py:516
Async XLA Ops:
  80.7 1.1 %copy-start = (f32[1472,128]{1,0:T(8,128)S(1)}, f32[1472,128]{1,0:T(8,128)}, u32[]{:S(2)}) copy-start(f32[1472,128]{1,0:T(8,128)} %program.1.parts_ref) | copy-start | bytes 2260996

commit v7 on v6

--- a/solution.py
+++ b/solution.py
@@ -314,9 +314,9 @@
     get_phi.start()
     get_a = pltpu.make_async_copy(a_h.at[:, 0, :], a_v, dsems.at[3])
     get_n = pltpu.make_async_copy(n_h.at[:, 0, :], n_v, dsems.at[4])
+    get_a.start()
     get_load.start()
     get_di.start()
-    get_a.start()
     get_n.start()
     sem = pltpu.get_barrier_semaphore()
     everyone(lambda device: pl.semaphore_signal(sem, inc=1, device_id=device, device_id_type=MESH))
@@ -341,6 +341,16 @@
     phi8 = jnp.concatenate([phi] * 8, axis=0)
     p24 = pick_cols(phi, pb)
     p64 = pick(s64_ref[...].astype(BF16), p24)
+    get_a.wait()
+    border_rows(a_v, arows)
+    ab = arows[...]
+    k64 = dot(p64, dot(ab, phi8, 1, 1)) * tmask_ref[...]
+    ksend[...] = pick_right(k64, spread_ref[...].astype(BF16))
+    pl.semaphore_wait(sem, GX * GY * GZ - 1)
+    owner_start(ksend, krecv, sems, 0)
+    fence()
+    near, pk = choose(nearcol, NI), choose(kcol, NB)
+    pkt = (lax.broadcasted_iota(jnp.int32, (NB, NS), 0) == krow[...]).astype(F32).astype(BF16)
     get_load.wait()
     lb_v[pl.ds(NB - 8, 8), :] = jnp.zeros((8, RHS), F32)
     for i, j, parts in SPLIT:
@@ -349,16 +359,6 @@
     lb, li = lb_v[...], li_v[...]
     get_di.wait()
     start = dot6(pieces(di_v[...]), li)
-    get_a.wait()
-    border_rows(a_v, arows)
-    ab = arows[...]
-    k64 = dot(p64, dot(ab, phi8, 1, 1)) * tmask_ref[...]
-    ksend[...] = pick_right(k64, spread_ref[...].astype(BF16))
-    pl.semaphore_wait(sem, GX * GY * GZ - 1)
-    owner_start(ksend, krecv, sems, 0)
-    fence()
-    near, pk = choose(nearcol, NI), choose(kcol, NB)
-    pkt = (lax.broadcasted_iota(jnp.int32, (NB, NS), 0) == krow[...]).astype(F32).astype(BF16)
 
     spot = lax.broadcasted_iota(jnp.int32, (NB, NODES), 1) == nearnode[...]
     tie = jnp.sum(jnp.where(spot, ab, 0.0), axis=1, keepdims=True)

time: 83.2 us -> 82.9 us (level)
  no operation moved by 1% of the time
where the time goes in v7:
time: 82.9 us; the launch traced here: 82.7 us
  Pallas kernels  81 us (98%)
  local copies, waits for them, and re-layouts  1.11 us (1%)
    pallas_call x1, Pallas kernels, local(): pl.pallas_call(program, out_shape=jax.ShapeDtypeStruct((2 * NB + 688, RHS...  79.8 us

profile of v7, /device:TPU:1, one launch (start us, length us, event | category | flops | bytes accessed | tf_op | source)
XLA Modules:
  0.0 82.7 jit_solution(4505284652752592089)
XLA Ops:
  0.6 79.8 %program.1.parts_ref = f32[1472,128]{1,0:T(8,128)} custom-call(f32[9,9,9,128]{3,2,1,0:T(8,128)} %load_h.1, f32[729,1,729]{2,1,0:T(1,128)} %bitcast.4, f32[343,1,343]{2,1,0:T(1,128)} %bitcast.6, f32[729,1,729]{2,1,0:T(1,128)} %bitcast.5, f32[20,1,729]{2,1,0:T(1,128)} %bitcast.7, s32[392,1]{1,0:T(8,128)} %constant.18.clone.bcol, ...), custom_call_target="tpu_custom_call" | custom-call | tf_op jit(solution)/shard_map/program/pallas_call | solution.py:501
  80.4 0.0 copy-start
  80.4 1.1 %copy-done = f32[1472,128]{1,0:T(8,128)S(1)} copy-done((f32[1472,128]{1,0:T(8,128)S(1)}, f32[1472,128]{1,0:T(8,128)}, u32[]{:S(2)}) %copy-start) | copy-done | bytes 753688
  81.5 1.2 %spread.1 = (f32[9,9,9,128]{3,2,1,0:T(8,128)}, f32[9,9,9,128]{3,2,1,0:T(8,128)}) custom-call(f32[1472,128]{1,0:T(8,128)S(1)} %copy-done), custom_call_target="tpu_custom_call" | custom-call | tf_op jit(solution)/shard_map/spread/pallas_call | solution.py:516
Async XLA Ops:
  80.4 1.1 %copy-start = (f32[1472,128]{1,0:T(8,128)S(1)}, f32[1472,128]{1,0:T(8,128)}, u32[]{:S(2)}) copy-start(f32[1472,128]{1,0:T(8,128)} %program.1.parts_ref) | copy-start | bytes 2260996
